TPU v7x, 256 devices: a whole 4x4x8 slice. The times are simulated.
256 devices in a mesh: ctx: 32 (over x, z), head: 8 (over y, core).
Axes of the slice: x: 4, y: 4, z: 8, core: 2. Of those that a mesh axis runs over, the one named last changes fastest.
Arguments:
- keys: bfloat16 [65536, 5120], P('ctx', 'head'), may hold values from -6 to 6
- values: bfloat16 [65536, 5120], P('ctx', 'head'), may hold values from -6 to 6
- queries: bfloat16 [65536, 5120], P('ctx', 'head'), may hold values from -6 to 6
- rates: float32 [65536, 16], P('ctx', 'head'), may hold values from 9.765625e-05 to 0.0009765625
- w_gate: bfloat16 [320, 16, 320], P('ctx', 'head'), may hold values from -0.3125 to 0.3125
- w_up: bfloat16 [320, 16, 320], P('ctx', 'head'), may hold values from -0.3125 to 0.3125
- w_down: bfloat16 [320, 16, 320], P('ctx', 'head'), may hold values from -0.3125 to 0.3125
- gain: float32 [5120], P('head'), may hold values from 0.5 to 1.5
Outputs:
- output: bfloat16 [65536, 5120], P('ctx', 'head')
- new_gate: bfloat16 [320, 16, 320], P('ctx', 'head')
- new_up: bfloat16 [320, 16, 320], P('ctx', 'head')
- new_down: bfloat16 [320, 16, 320], P('ctx', 'head')
All inputs are finite; a program needn't handle non-finite values.
Results may differ from a plain program's by a relative error of at most 0.0092.
Values may be sent and summed in bfloat16 or wider, within the bound.
No kernel may reach another device: no remote copies, remote signals or barrier semaphores. Data moves between devices by JAX's collectives and lax.ppermute only.
A program may use at most 128 MiB of HBM per device.

v0:
```python
import jax
import jax.numpy as jnp
from jax import lax
from jax.sharding import PartitionSpec as P

HEADS = 16
DH = 320
EPS = 1e-06


def joined_along(pieces, dim):
    dims = list(pieces.shape[1:])
    dims[dim] *= pieces.shape[0]
    return jnp.moveaxis(pieces, 0, dim).reshape(dims)


def from_everyone(array, axis):
    peers = lax.axis_size(axis)
    return lax.all_to_all(
        jnp.broadcast_to(array[None], (peers, *array.shape)), axis, 0, 0, tiled=True
    )


def gather_directly(array, axis, dim):
    return joined_along(from_everyone(array, axis), dim)


def sent_together(arrays, axis, dim, along):
    ends, at = ([], 0)
    for a in arrays[:-1]:
        at += a.shape[along]
        ends.append(at)
    both = jnp.concatenate(arrays, axis=along)
    return tuple(jnp.split(gather_directly(both, axis, dim), ends, axis=along))


def taken_together(array, axis):
    everything = from_everyone(array, axis)
    return jnp.sum(everything, axis=0)


def per_device(keys, values, queries, rates, w_gate, w_up, w_down, gain):
    rows = keys.shape[0]
    heads = w_gate.shape[1]
    width = w_gate.shape[2]
    local_units = w_gate.shape[0]
    keyh = keys.reshape(rows, heads, width)
    valueh = values.reshape(rows, heads, width)
    queryh = queries.reshape(rows, heads, width)
    full_gate, full_up, full_down = sent_together((w_gate, w_up, w_down), "ctx", 0, 1)
    gpre = jnp.einsum("thd,fhd->thf", keyh, full_gate, preferred_element_type=jnp.float32)
    upre = jnp.einsum("thd,fhd->thf", keyh, full_up, preferred_element_type=jnp.float32)
    sig = jax.nn.sigmoid(gpre)
    act = gpre * sig
    slope = sig * (1.0 + gpre * (1.0 - sig))
    hidden = (act * upre).astype(jnp.bfloat16)
    scaled = (valueh.astype(jnp.float32) * rates[:, :, None]).astype(jnp.bfloat16)
    back = jnp.einsum("thd,fhd->thf", scaled, full_down, preferred_element_type=jnp.float32)
    dgate = (back * upre * slope).astype(jnp.bfloat16)
    dup = (back * act).astype(jnp.bfloat16)
    grad_gate = jnp.einsum("thf,thd->fhd", dgate, keyh, preferred_element_type=jnp.float32)
    grad_up = jnp.einsum("thf,thd->fhd", dup, keyh, preferred_element_type=jnp.float32)
    grad_down = jnp.einsum("thf,thd->fhd", hidden, scaled, preferred_element_type=jnp.float32)
    total = lax.psum(jnp.stack([grad_gate, grad_up, grad_down], axis=1), "ctx")
    olds = jnp.stack([full_gate, full_up, full_down], axis=1).astype(jnp.float32)
    updated = olds + total
    old_sq = jnp.sum(olds * olds, axis=0)
    new_sq = jnp.sum(updated * updated, axis=0)
    fresh = (updated * (jnp.sqrt(old_sq) * lax.rsqrt(new_sq + EPS))[None]).astype(jnp.bfloat16)
    offset = lax.axis_index("ctx") * local_units
    mine = lax.dynamic_slice_in_dim(fresh, offset, local_units, 0)
    new_gate = fresh[:, 0]
    new_up = fresh[:, 1]
    new_down = fresh[:, 2]
    qgate = jnp.einsum("thd,fhd->thf", queryh, new_gate, preferred_element_type=jnp.float32)
    qup = jnp.einsum("thd,fhd->thf", queryh, new_up, preferred_element_type=jnp.float32)
    mixed = (jax.nn.silu(qgate) * qup).astype(jnp.bfloat16)
    outh = jnp.einsum("thf,fhd->thd", mixed, new_down, preferred_element_type=jnp.float32)
    squares = taken_together(jnp.sum(outh * outh, axis=(1, 2)), "head")
    scale = lax.rsqrt(squares / (HEADS * DH) + EPS)
    result = outh * scale[:, None, None] * gain.reshape(heads, width)[None]
    output = result.reshape(rows, heads * width).astype(jnp.bfloat16)
    return (output, mine[:, 0], mine[:, 1], mine[:, 2])


def solution(mesh):
    in_specs = (
        P("ctx", "head"),
        P("ctx", "head"),
        P("ctx", "head"),
        P("ctx", "head"),
        P("ctx", "head", None),
        P("ctx", "head", None),
        P("ctx", "head", None),
        P("head"),
    )
    out_specs = (
        P("ctx", "head"),
        P("ctx", "head", None),
        P("ctx", "head", None),
        P("ctx", "head", None),
    )
    return jax.shard_map(
        per_device, mesh=mesh, in_specs=in_specs, out_specs=out_specs, check_vma=False
    )
```

profile of v0, /device:TPU:1, one launch (start us, length us, event | category | flops | bytes accessed | tf_op | source)
XLA Modules:
  0.0 292.5 jit_solution(10349840413681517928)
XLA Ops:
  7.2 0.8 pad_maximum_fusion.2
  8.0 1.4 broadcast_in_dim.4
  9.4 12.0 %all-to-all-start = ((bf16[32,10,6,320]{3,2,1,0:T(8,128)(2,1)}), bf16[32,10,6,320]{3,2,1,0:T(8,128)(2,1)}, u32[]{:S(2)}, u32[]{:S(2)}) async-start(bf16[32,10,6,320]{3,2,1,0:T(8,128)(2,1)} %broadcast_in_dim.4), calls=%async_computation | async-start | bytes 3932160 | tf_op jit(solution)/shard_map/all_to_all | solution.py:19
  21.4 0.0 all-reduce.2.cloned.1.call-start
  21.4 3.0 %copy.53 = bf16[2048,640]{0,1:T(8,128)(2,1)S(1)} copy(bf16[2048,640]{1,0:T(8,128)(2,1)} %param.8) | data formatting | bytes 5242880 | tf_op args[0]
  24.4 4.4 %copy.52 = bf16[2048,640]{0,1:T(8,128)(2,1)} copy(bf16[2048,640]{1,0:T(8,128)(2,1)} %param.9) | data formatting | bytes 5242880 | tf_op args[1]
  28.8 38.8 %all-to-all-done = bf16[32,10,6,320]{3,2,1,0:T(8,128)(2,1)} async-done(((bf16[32,10,6,320]{3,2,1,0:T(8,128)(2,1)}), bf16[32,10,6,320]{3,2,1,0:T(8,128)(2,1)}, u32[]{:S(2)}, u32[]{:S(2)}) %all-to-all-start) | async-done | bytes 1228832 | tf_op jit(solution)/shard_map/all_to_all | solution.py:19
  67.6 4.1 %fusion.46 = (bf16[320,2,320]{2,1,0:T(2,128)(2,1)S(1)}, bf16[320,2,320]{2,1,0:T(2,128)(2,1)S(1)}, bf16[320,2,320]{2,1,0:T(2,128)(2,1)S(1)}) fusion(bf16[320,6,320]{2,1,0:T(8,128)(2,1)} %bitcast), kind=kLoop, calls=%fused_computation.63 | loop fusion | bytes 2457600 | tf_op jit(solution)/shard_map/split | solution.py:34
  71.8 0.0 copy-start.4
  71.8 0.0 copy-start.3
  71.8 1.5 fusion.40
  73.3 0.0 copy-done.4
  73.3 0.0 copy-start.1
  73.3 0.0 copy-start.10
  73.4 3.8 %fusion.38 = f32[2,320,2048]{2,1,0:T(8,128)} fusion(bf16[2048,2,320]{0,2,1:T(8,128)(2,1)S(1)} %bitcast.134, bf16[320,2,320]{2,1,0:T(2,128)(2,1)S(1)} %get-tuple-element.23), kind=kOutput, calls=%fused_computation.47 | convolution fusion | flops 838860800 | bytes 8273920 | tf_op jit(solution)/shard_map/thd,fhd->thf/dot_general | solution.py:52
  77.2 0.0 copy-done.3
  77.2 0.0 copy-done.1
  77.2 0.0 copy-done.10
  77.2 1.5 fusion.22
  78.7 0.0 copy-start.2
  78.7 2.3 copy-done.2
  81.1 1.7 fusion.33
  82.7 7.2 %fusion.25 = f32[320,1,2,320]{3,0,2,1:T(8,128)} fusion(bf16[2048,2,320]{0,2,1:T(8,128)(2,1)S(1)} %bitcast.136, f32[2,320,2048]{2,1,0:T(8,128)S(1)} %fusion.40, f32[2,320,2048]{2,1,0:T(8,128)} %fusion.38, f32[2,320,2048]{2,1,0:T(8,128)} %copy-done.2), kind=kOutput, calls=%fused_computation.38 | convolution fusion | flops 851968000 | bytes 19169280 | tf_op jit(solution)/shard_map/thf,thd->fhd/dot_general | solution.py:61
  89.9 0.0 copy-start.9
  89.9 4.3 %fusion.28 = f32[320,1,2,320]{3,0,2,1:T(8,128)S(1)} fusion(f32[2,320,2048]{2,1,0:T(8,128)} %fusion.38, bf16[2048,2,320]{0,2,1:T(8,128)(2,1)S(1)} %bitcast.140, f32[2048,2]{0,1:T(2,128)S(1)} %copy-done.10, f32[2,320,2048]{2,1,0:T(8,128)S(1)} %fusion.40), kind=kOutput, calls=%fused_computation.39 | convolution fusion | flops 850657280 | bytes 13942784 | tf_op jit(solution)/shard_map/thf,thd->fhd/dot_general | solution.py:63
  94.2 0.0 copy-done.9
  94.2 1.8 pad_maximum_fusion
  96.0 0.0 all-reduce.2.cloned.1.call-update
  96.0 0.0 copy-start.11
  96.1 3.2 %copy.55 = bf16[2048,640]{0,1:T(8,128)(2,1)S(1)} copy(bf16[2048,640]{1,0:T(8,128)(2,1)} %param.10) | data formatting | bytes 5242880 | tf_op args[2]
  99.2 0.0 copy-done.11
  99.3 0.1 mul.103
  99.3 0.8 copy.77
  100.2 0.0 copy-start.5
  100.2 2.3 copy_bitcast_fusion
  102.5 146.1 %all-reduce.2.cloned.1.call-done = f32[320,3,2,320]{3,0,2,1:T(8,128)} async-done(((f32[320,3,2,320]{3,0,2,1:T(8,128)}), f32[320,3,2,320]{3,0,2,1:T(8,128)}) %all-reduce.2.cloned.1.call-update) | async-done | bytes 2457616 | tf_op jit(solution)/shard_map/psum | solution.py:64
  248.6 0.0 copy-start
  248.6 0.0 copy-start.6
  248.6 0.0 copy-start.7
  248.6 3.1 %fusion.14 = (f32[3,2,320]{2,1,0:T(2,128)S(1)}, f32[3,2,320]{2,1,0:T(2,128)S(1)}) fusion(bf16[320,1,2,320]{3,0,2,1:T(8,128)(2,1)} %get-tuple-element.30, bf16[320,1,2,320]{3,0,2,1:T(8,128)(2,1)} %get-tuple-element.31, bf16[320,1,2,320]{3,0,2,1:T(8,128)(2,1)} %bitcast.142, f32[320,3,2,320]{3,0,2,1:T(8,128)} %all-reduce.2.cloned.1.call-done), kind=kLoop, calls=%fused_computation.28 | loop fusion | flops 4911360 | bytes 3701760 | tf_op jit(solution)/shard_map/reduce_sum | solution.py:67
  251.8 0.0 copy-done.5
  251.8 0.0 copy-done
  251.8 0.1 copy-done.6
  251.9 0.1 copy-done.7
  252.0 0.5 multiply_convert_fusion.1
  252.5 0.0 copy-start.8
  252.5 1.1 copy-done.8
  253.6 3.9 %fusion.36 = f32[2,320,2048]{2,1,0:T(8,128)} fusion(bf16[2048,2,320]{0,2,1:T(8,128)(2,1)S(1)} %bitcast.137, bf16[320,3,2,320]{3,0,2,1:T(8,128)(2,1)S(1)} %multiply_convert_fusion.1), kind=kOutput, calls=%fused_computation.43 | convolution fusion | flops 838860800 | bytes 8355840 | tf_op jit(solution)/shard_map/thd,fhd->thf/dot_general | solution.py:75
  257.5 8.4 %multiply_reduce_fusion = (f32[2048]{0:T(1024)S(1)}, f32[2,320,2048]{2,1,0:T(8,128)}) fusion(f32[2,320,2048]{2,1,0:T(8,128)} %fusion.36, bf16[2048,2,320]{0,2,1:T(8,128)(2,1)S(1)} %bitcast.138, bf16[320,3,2,320]{3,0,2,1:T(8,128)(2,1)} %copy-done.8), kind=kOutput, calls=%fused_computation.25 | convolution fusion | flops 1688205312 | bytes 14098432 | tf_op jit(solution)/shard_map/thf,fhd->thd/dot_general | solution.py:78
  265.9 0.6 broadcast_in_dim.5
  266.6 8.6 %all-to-all-start.1 = ((f32[8,1,2048]{2,1,0:T(1,128)}), f32[8,1,2048]{2,1,0:T(1,128)S(1)}, u32[]{:S(2)}, u32[]{:S(2)}) async-start(f32[8,1,2048]{2,1,0:T(1,128)} %broadcast_in_dim.5), calls=%async_computation.1 | async-start | bytes 131072 | tf_op jit(solution)/shard_map/all_to_all | solution.py:19
  275.2 0.8 dynamic-slice_bitcast_fusion
  276.0 0.6 copy.59
  276.6 0.6 copy.60
  277.3 0.6 copy.61
  277.9 2.2 all-to-all-done.1
  280.0 0.1 reduce_sum.39
  280.1 3.0 %multiply_convert_fusion = bf16[2,320,2048]{2,1,0:T(8,128)(2,1)S(1)} fusion(f32[2,320,2048]{2,1,0:T(8,128)} %get-tuple-element.29, f32[2,320]{1,0:T(2,128)S(1)} %mul.103, f32[2048]{0:T(1024)S(1)} %add_rsqrt_fusion), kind=kLoop, calls=%fused_computation.24 | loop fusion | flops 3932160 | bytes 7875072 | tf_op jit(solution)/shard_map/convert_element_type | solution.py:82
  283.1 2.6 copy.58
  (2 shorter events, 0.0 us)
Async XLA Ops:
  9.4 58.2 %all-to-all-start = ((bf16[32,10,6,320]{3,2,1,0:T(8,128)(2,1)}), bf16[32,10,6,320]{3,2,1,0:T(8,128)(2,1)}, u32[]{:S(2)}, u32[]{:S(2)}) async-start(bf16[32,10,6,320]{3,2,1,0:T(8,128)(2,1)} %broadcast_in_dim.4), calls=%async_computation | async-start | bytes 3932160 | tf_op jit(solution)/shard_map/all_to_all | solution.py:19
  21.4 227.2 %all-reduce.2.cloned.1.call-start = ((), (), s32[]{:S(2)}) async-start(), calls=%async_computation.2 | async-start | bytes 5898240 | tf_op jit(solution)/shard_map/psum | solution.py:64
  71.8 1.6 copy-start.4
  71.8 5.4 %copy-start.3 = (bf16[320,2,320]{2,1,0:T(2,128)(2,1)}, bf16[320,2,320]{2,1,0:T(2,128)(2,1)S(1)}, u32[]{:S(2)}) copy-start(bf16[320,2,320]{2,1,0:T(2,128)(2,1)S(1)} %get-tuple-element.22) | copy-start | bytes 1228804
  73.3 3.8 %copy-start.1 = (bf16[2048,640]{0,1:T(8,128)(2,1)S(1)}, bf16[2048,640]{0,1:T(8,128)(2,1)}, u32[]{:S(2)}) copy-start(bf16[2048,640]{0,1:T(8,128)(2,1)} %copy.52) | copy-start | bytes 7864324
  73.3 3.8 %copy-start.10 = (f32[2048,2]{0,1:T(2,128)S(1)}, f32[2048,2]{0,1:T(2,128)}, u32[]{:S(2)}) copy-start(f32[2048,2]{0,1:T(2,128)} %param.11) | copy-start | bytes 49156
  78.7 2.3 copy-start.2
  89.9 4.3 %copy-start.9 = (f32[320,1,2,320]{3,0,2,1:T(8,128)S(1)}, f32[320,1,2,320]{3,0,2,1:T(8,128)}, u32[]{:S(2)}) copy-start(f32[320,1,2,320]{3,0,2,1:T(8,128)} %fusion.25) | copy-start | bytes 2457604
  96.0 3.2 %copy-start.11 = (f32[640]{0:T(1024)S(1)}, f32[640]{0:T(1024)}, u32[]{:S(2)}) copy-start(f32[640]{0:T(1024)} %param.15) | copy-start | bytes 7684
  100.2 151.6 %copy-start.5 = (bf16[320,2,320]{2,0,1:T(8,128)(2,1)S(1)}, bf16[320,2,320]{2,0,1:T(8,128)(2,1)}, u32[]{:S(2)}) copy-start(bf16[320,2,320]{2,0,1:T(8,128)(2,1)} %copy.77) | copy-start | bytes 1228804
  248.6 3.2 %copy-start = (f32[320,3,2,320]{3,0,2,1:T(8,128)S(1)}, f32[320,3,2,320]{3,0,2,1:T(8,128)}, u32[]{:S(2)}) copy-start(f32[320,3,2,320]{3,0,2,1:T(8,128)} %all-reduce.2.cloned.1.call-done) | copy-start | bytes 7372804
  248.6 3.2 %copy-start.6 = (bf16[320,1,2,320]{3,0,2,1:T(8,128)(2,1)S(1)}, bf16[320,1,2,320]{3,0,2,1:T(8,128)(2,1)}, u32[]{:S(2)}) copy-start(bf16[320,1,2,320]{3,0,2,1:T(8,128)(2,1)} %get-tuple-element.30) | copy-start | bytes 1228804
  248.6 3.4 %copy-start.7 = (bf16[320,1,2,320]{3,0,2,1:T(8,128)(2,1)S(1)}, bf16[320,1,2,320]{3,0,2,1:T(8,128)(2,1)}, u32[]{:S(2)}) copy-start(bf16[320,1,2,320]{3,0,2,1:T(8,128)(2,1)} %get-tuple-element.31) | copy-start | bytes 1228804
  252.5 1.1 copy-start.8
  266.6 13.5 %all-to-all-start.1 = ((f32[8,1,2048]{2,1,0:T(1,128)}), f32[8,1,2048]{2,1,0:T(1,128)S(1)}, u32[]{:S(2)}, u32[]{:S(2)}) async-start(f32[8,1,2048]{2,1,0:T(1,128)} %broadcast_in_dim.5), calls=%async_computation.1 | async-start | bytes 131072 | tf_op jit(solution)/shard_map/all_to_all | solution.py:19
Sparse Core Ops, SparseCore 0:
  96.2 152.3 all-reduce.1
where the time goes:
time: 293 us
  waiting for transfers between devices  187 us (64%)
  matrix products  32.3 us (11%)
  local copies, waits for them, and re-layouts  28.9 us (10%)
  starting transfers between devices  20.6 us (7%)
  between operations  14.2 us (5%)
  other arithmetic  9.31 us (3%)
    psum x1, waiting for transfers between devices, per_device(): total = lax.psum(jnp.stack([grad_gate, grad_up, grad_down], axis=1), 'ctx')  146 us
    all_to_all x2, waiting for transfers between devices, from_everyone(): lax.all_to_all(jnp.broadcast_to(array[None], (peers, *array.shape)), axis...  41 us
    all_to_all x2, starting transfers between devices, from_everyone(): lax.all_to_all(jnp.broadcast_to(array[None], (peers, *array.shape)), axis...  20.6 us
    unnamed x32, local copies, waits for them, and re-layouts  19.5 us
    dot_general x1, matrix products, per_device(): jnp.einsum('thf,fhd->thd', mixed, new_down, preferred_element_type=jnp.fl...  8.44 us
    dot_general x1, matrix products, per_device(): jnp.einsum('thf,thd->fhd', dgate, keyh, preferred_element_type=jnp.float32)  7.15 us
  transfers between devices with their start and end apart: 3, of which 3 were waited for; matrix products, arithmetic and copies ran while one was open for 6% of the time, Pallas kernels for 0%

commit v1 on v0

--- a/solution.py
+++ b/solution.py
@@ -40,6 +40,12 @@
 
 
 def per_device(keys, values, queries, rates, w_gate, w_up, w_down, gain):
+
+    def pass_the_numbers(panel, shard_axis):
+        w2 = lax.all_gather(panel, shard_axis)
+        h_now = jnp.sum(w2, axis=0)
+        return h_now
+
     rows = keys.shape[0]
     heads = w_gate.shape[1]
     width = w_gate.shape[2]
@@ -61,7 +67,7 @@
     grad_gate = jnp.einsum("thf,thd->fhd", dgate, keyh, preferred_element_type=jnp.float32)
     grad_up = jnp.einsum("thf,thd->fhd", dup, keyh, preferred_element_type=jnp.float32)
     grad_down = jnp.einsum("thf,thd->fhd", hidden, scaled, preferred_element_type=jnp.float32)
-    total = lax.psum(jnp.stack([grad_gate, grad_up, grad_down], axis=1), "ctx")
+    total = pass_the_numbers(jnp.stack([grad_gate, grad_up, grad_down], axis=1), "ctx")
     olds = jnp.stack([full_gate, full_up, full_down], axis=1).astype(jnp.float32)
     updated = olds + total
     old_sq = jnp.sum(olds * olds, axis=0)

time: 293 us -> 757 us (2.58)
  waiting for transfers between devices: 187 us -> 626 us
  other arithmetic: 9.31 us -> 37.4 us
    all_gather x0 -> x1, waiting for transfers between devices: none -> 585 us  [pass_the_numbers(): w2 = lax.all_gather(panel, shard_axis)]
    psum x1 -> x0, waiting for transfers between devices: 146 us -> none  [per_device(): total = lax.psum(jnp.stack([grad_gate, grad_up, grad_down], axis=1), 'ctx')]
    reduce_sum x0 -> x1, other arithmetic: none -> 29.2 us  [pass_the_numbers(): h_now = jnp.sum(w2, axis=0)]
    unnamed x32 -> x38, local copies, waits for them, and re-layouts: 19.5 us -> 21.3 us
  transfers between devices with their start and end apart: 3 -> 3, of which waited for: 3 -> 3; matrix products, arithmetic and copies ran while one was open for 6% -> 2% of each run, Pallas kernels for 0% -> 0%
where the time goes in v1:
time: 757 us; the launch traced here: 756 us
  waiting for transfers between devices  626 us (83%)
  other arithmetic  37.4 us (5%)
  matrix products  32.3 us (4%)
  local copies, waits for them, and re-layouts  29.5 us (4%)
  starting transfers between devices  17.3 us (2%)
  between operations  14.3 us (2%)
    all_gather x1, waiting for transfers between devices, pass_the_numbers(): w2 = lax.all_gather(panel, shard_axis)  585 us
    all_to_all x2, waiting for transfers between devices, from_everyone(): lax.all_to_all(jnp.broadcast_to(array[None], (peers, *array.shape)), axis...  41 us
    reduce_sum x1, other arithmetic, pass_the_numbers(): h_now = jnp.sum(w2, axis=0)  29.2 us
    unnamed x38, local copies, waits for them, and re-layouts  21.3 us
    all_to_all x2, starting transfers between devices, from_everyone(): lax.all_to_all(jnp.broadcast_to(array[None], (peers, *array.shape)), axis...  17.3 us
  transfers between devices with their start and end apart: 3, of which 3 were waited for; matrix products, arithmetic and copies ran while one was open for 2% of the time, Pallas kernels for 0%

profile of v1, /device:TPU:1, one launch (start us, length us, event | category | flops | bytes accessed | tf_op | source)
XLA Modules:
  0.0 756.5 jit_solution(14609785470190497737)
XLA Ops:
  7.2 0.8 pad_maximum_fusion.2
  8.0 1.4 broadcast_in_dim.4
  9.4 12.0 %all-to-all-start = ((bf16[32,10,6,320]{3,2,1,0:T(8,128)(2,1)}), bf16[32,10,6,320]{3,2,1,0:T(8,128)(2,1)}, u32[]{:S(2)}, u32[]{:S(2)}) async-start(bf16[32,10,6,320]{3,2,1,0:T(8,128)(2,1)} %broadcast_in_dim.4), calls=%async_computation | async-start | bytes 3932160 | tf_op jit(solution)/shard_map/all_to_all | solution.py:19
  21.4 0.0 all-gather.3.cloned.1.call-start
  21.4 3.0 copy.53
  24.4 4.4 copy.52
  28.8 38.8 %all-to-all-done = bf16[32,10,6,320]{3,2,1,0:T(8,128)(2,1)} async-done(((bf16[32,10,6,320]{3,2,1,0:T(8,128)(2,1)}), bf16[32,10,6,320]{3,2,1,0:T(8,128)(2,1)}, u32[]{:S(2)}, u32[]{:S(2)}) %all-to-all-start) | async-done | bytes 1228832 | tf_op jit(solution)/shard_map/all_to_all | solution.py:19
  67.6 4.2 fusion.46
  71.8 0.0 copy-start.6
  71.8 0.0 copy-start.4
  71.8 1.5 fusion.40
  73.3 0.0 copy-done.6
  73.3 0.0 copy-start.2
  73.3 0.0 copy-start.13
  73.4 3.8 fusion.38
  77.2 0.0 copy-done.4
  77.2 0.0 copy-done.2
  77.2 0.0 copy-done.13
  77.2 1.5 fusion.22
  78.8 0.0 copy-start.3
  78.8 2.3 copy-done.3
  81.1 1.7 fusion.33
  82.8 7.1 fusion.25
  89.9 0.0 copy-start.12
  89.9 4.3 fusion.28
  94.2 0.0 copy-done.12
  94.2 1.9 pad_maximum_fusion
  96.2 0.0 all-gather.3.cloned.1.call-update
  96.2 0.0 copy-start.14
  96.2 0.0 copy-start.5
  96.2 0.0 copy-start.7
  96.2 4.5 copy.55
  100.7 0.0 copy-done.14
  100.7 0.1 mul.103
  100.8 0.9 copy.77
  101.6 0.0 copy-done.5
  101.7 0.0 copy-done.7
  101.7 1.1 copy_bitcast_fusion
  102.7 584.7 %all-gather.3.cloned.1.call-done = f32[10240,3,2,320]{3,0,2,1:T(8,128)} async-done(((f32[320,3,2,320]{3,0,2,1:T(8,128)}), f32[10240,3,2,320]{3,0,2,1:T(8,128)}) %all-gather.3.cloned.1.call-update) | async-done | bytes 78643216 | tf_op jit(solution)/shard_map/all_gather | solution.py:45
  687.4 29.2 %reduce_sum.45 = f32[320,3,2,320]{3,0,2,1:T(8,128)S(1)} reduce(f32[32,320,3,2,320]{4,1,0,3,2:T(8,128)} %bitcast.15, f32[]{:T(128)} %constant.10.clone.1), dimensions={0}, to_apply=%region_0.0 | reduce | flops 19046400 | bytes 81100800 | tf_op jit(solution)/shard_map/reduce_sum | solution.py:46
  716.5 0.0 copy-start.9
  716.5 0.0 copy-start.10
  716.6 0.0 copy-done.8
  716.6 2.0 fusion.14
  718.6 0.0 copy-done.9
  718.6 0.0 copy-done.10
  718.6 0.0 copy-start
  718.6 0.5 multiply_convert_fusion.1
  719.1 0.0 copy-start.11
  719.1 1.1 copy-done.11
  720.2 0.7 copy-done
  720.9 3.9 fusion.36
  724.7 0.0 copy-done.1
  724.7 8.4 %multiply_reduce_fusion = (f32[2048]{0:T(1024)S(1)}, f32[2,320,2048]{2,1,0:T(8,128)}) fusion(f32[2,320,2048]{2,1,0:T(8,128)} %fusion.36, bf16[2048,2,320]{0,2,1:T(8,128)(2,1)S(1)} %bitcast.139, bf16[320,3,2,320]{3,0,2,1:T(8,128)(2,1)} %copy-done.11), kind=kOutput, calls=%fused_computation.25 | convolution fusion | flops 1688205312 | bytes 14098432 | tf_op jit(solution)/shard_map/thf,fhd->thd/dot_general | solution.py:84
  733.2 0.7 broadcast_in_dim.5
  733.8 5.3 all-to-all-start.1
  739.2 0.8 dynamic-slice_bitcast_fusion
  740.0 0.6 copy.59
  740.6 0.6 copy.60
  741.2 0.6 copy.61
  741.8 2.2 all-to-all-done.1
  744.0 0.1 reduce_sum.49
  744.1 3.0 multiply_convert_fusion
  747.1 2.6 copy.58
  (4 shorter events, 0.0 us)
Async XLA Ops:
  9.4 58.2 %all-to-all-start = ((bf16[32,10,6,320]{3,2,1,0:T(8,128)(2,1)}), bf16[32,10,6,320]{3,2,1,0:T(8,128)(2,1)}, u32[]{:S(2)}, u32[]{:S(2)}) async-start(bf16[32,10,6,320]{3,2,1,0:T(8,128)(2,1)} %broadcast_in_dim.4), calls=%async_computation | async-start | bytes 3932160 | tf_op jit(solution)/shard_map/all_to_all | solution.py:19
  21.4 666.0 %all-gather.3.cloned.1.call-start = ((), (), s32[]{:S(2)}) async-start(), calls=%async_computation.2 | async-start | bytes 97320960 | tf_op jit(solution)/shard_map/all_gather | solution.py:45
  71.8 1.5 copy-start.6
  71.8 5.4 copy-start.4
  73.3 3.9 copy-start.2
  73.3 3.9 copy-start.13
  78.8 2.3 copy-start.3
  89.9 4.3 copy-start.12
  96.2 4.5 copy-start.14
  96.2 5.5 copy-start.5
  96.2 5.4 copy-start.7
  687.4 29.2 %copy-start.8 = (bf16[320,2,320]{2,0,1:T(8,128)(2,1)S(1)}, bf16[320,2,320]{2,0,1:T(8,128)(2,1)}, u32[]{:S(2)}) copy-start(bf16[320,2,320]{2,0,1:T(8,128)(2,1)} %copy.77) | copy-start | bytes 1228804
  716.5 2.0 copy-start.9
  716.5 2.0 copy-start.10
  718.6 2.3 copy-start
  719.1 1.1 copy-start.11
  720.9 3.9 copy-start.1
  733.8 10.2 %all-to-all-start.1 = ((f32[8,1,2048]{2,1,0:T(1,128)}), f32[8,1,2048]{2,1,0:T(1,128)S(1)}, u32[]{:S(2)}, u32[]{:S(2)}) async-start(f32[8,1,2048]{2,1,0:T(1,128)} %broadcast_in_dim.5), calls=%async_computation.1 | async-start | bytes 131072 | tf_op jit(solution)/shard_map/all_to_all | solution.py:19
Sparse Core Ops, SparseCore 0:
  96.3 591.0 all-gather.2
